TPU v7x, 256 devices: a whole 4x4x8 slice. The times are simulated.
256 devices in a mesh: chan: 64 (over y, x_hi, z), blk: 4 (over x_lo, core).
Axes of the slice: x: 4 (x_hi: 2, x_lo: 2; x = x_hi * 2 + x_lo), y: 4, z: 8, core: 2. Of those that a mesh axis runs over, the one named last changes fastest.
Arguments:
- voltages: int32 [1024, 262144], P('chan', 'blk'), may hold values from -127 to 127, as said below
Outputs:
- vis_real: float32 [256, 1024, 1024], P(('chan', 'blk'))
- vis_imag: float32 [256, 1024, 1024], P(('chan', 'blk'))
Inputs may be any that keep to these rules, and one draw needn't show every extreme that they name: `voltages`: integer voltage samples.
All inputs are finite; a program needn't handle non-finite values.
Results may differ from a plain program's by a relative error of at most 0.004.
Values may be sent and summed in bfloat16 or wider, within the bound.
A program may use at most 64 MiB of HBM per device.

v0:
```python
import jax
import jax.numpy as jnp
from jax import lax
from jax.sharding import PartitionSpec as P

NI = 1024
NC = 256
TAPS = 4
FFT = 512


def shifted(value, axis, steps):
    count = lax.axis_size(axis)
    leading, last = (max(0, -steps), min(count, count - steps))
    return lax.ppermute(value, axis, [(source, source + steps) for source in range(leading, last)])


def build_taps():
    length = TAPS * FFT
    points = jnp.arange(length, dtype=jnp.float32)
    centre = (length - 1) / 2.0
    window = 0.54 - 0.46 * jnp.cos(2.0 * jnp.pi * points / (length - 1))
    return (jnp.sinc((points - centre) / FFT) * window).reshape(TAPS, FFT)


def spectrum_scale(filter_taps):
    energy = jnp.mean(jnp.sum(filter_taps * filter_taps, axis=0))
    return 1.0 / (56.0 * jnp.sqrt(FFT * energy))


def build_transform():
    points = jnp.arange(FFT, dtype=jnp.int32)[:, None]
    column = jnp.arange(NC, dtype=jnp.int32)
    angle = (points * column[None, :] % FFT).astype(jnp.float32) * (2.0 * jnp.pi / FFT)
    return jnp.concatenate([jnp.cos(angle), -jnp.sin(angle)], axis=1)


def apply_taps(padded, filter_taps, frames_dev):
    filtered = filter_taps[0] * padded[:, 0:frames_dev, :]
    for offset in range(1, TAPS):
        filtered = filtered + filter_taps[offset] * padded[:, offset : offset + frames_dev, :]
    return filtered


def to_spectra(filtered, transform, scale_factor):
    inputs_here = filtered.shape[0]
    frames_dev = filtered.shape[1]
    spectra = (
        jnp.einsum("ifn,nk->kif", filtered, transform, precision=lax.Precision.HIGHEST)
        * scale_factor
    )
    spectra = spectra.reshape(2, NC, inputs_here, frames_dev).transpose(1, 2, 0, 3)
    return spectra.reshape(NC, inputs_here, 2 * frames_dev).astype(jnp.bfloat16)


def local(voltages):
    inputs_here = voltages.shape[0]
    frames_dev = voltages.shape[1] // FFT
    chan_count = lax.axis_size("chan")
    blk_count = lax.axis_size("blk")
    chan_local = NC // (chan_count * blk_count)
    filter_taps = build_taps()
    scale_factor = spectrum_scale(filter_taps)
    history_len = TAPS - 1
    samples = voltages.astype(jnp.float32).reshape(inputs_here, frames_dev, FFT)
    tail = voltages[:, (frames_dev - history_len) * FFT :].astype(jnp.bfloat16)
    earlier = shifted(tail, "blk", 1)
    earlier = earlier.astype(jnp.float32).reshape(inputs_here, history_len, FFT)
    padded = jnp.concatenate([earlier, samples], axis=1)
    filtered = apply_taps(padded, filter_taps, frames_dev)
    spectra = to_spectra(filtered, build_transform(), scale_factor)
    turned = lax.all_to_all(
        lax.all_to_all(spectra, "chan", split_axis=0, concat_axis=1, tiled=True),
        "blk",
        split_axis=0,
        concat_axis=2,
        tiled=True,
    )
    stacked = turned.reshape(chan_local, NI, blk_count, 2, frames_dev)
    swapped = jnp.concatenate([stacked[:, :, :, 1:2], -stacked[:, :, :, 0:1]], axis=3)
    swapped = swapped.reshape(chan_local, NI, 2 * blk_count * frames_dev)
    total_frames = blk_count * frames_dev
    vis_real = (
        jnp.einsum("cim,cjm->cij", turned, turned, preferred_element_type=jnp.float32)
        / total_frames
    )
    vis_imag = (
        jnp.einsum("cim,cjm->cij", swapped, turned, preferred_element_type=jnp.float32)
        / total_frames
    )
    return (vis_real, vis_imag)


def solution(mesh):
    return jax.shard_map(
        local,
        mesh=mesh,
        in_specs=(P("chan", "blk"),),
        out_specs=(P(("chan", "blk"), None, None), P(("chan", "blk"), None, None)),
        check_vma=False,
    )
```

profile of v0, /device:TPU:1, one launch (start us, length us, event | category | flops | bytes accessed | tf_op | source)
XLA Modules:
  0.0 150.4 jit_solution(6807475328736510792)
XLA Ops:
  0.6 0.9 slice_convert_fusion
  1.5 4.5 %collective-permute-start = (bf16[16,1536]{1,0:T(8,128)(2,1)S(1)}, bf16[16,1536]{1,0:T(8,128)(2,1)S(1)}, u32[]{:S(2)}, u32[]{:S(2)}) collective-permute-start(bf16[16,1536]{1,0:T(8,128)(2,1)S(1)} %slice_convert_fusion), channel_id=1, source_target_pairs={{0,1},{1,2},{2,3},{4,5},{5,6},{6,7},{8,9},{9,10},{10,11},{12,13},{... | collective-permute-start | bytes 147464 | tf_op jit(solution)/shard_map/ppermute | solution.py:15
  6.0 0.1 fusion.35
  6.1 2.1 %sine_negate_fusion = (f32[512,256]{0,1:T(8,128)S(1)}, f32[512,256]{0,1:T(8,128)S(1)}) fusion(), kind=kLoop, calls=%fused_computation.36 | loop fusion | flops 1966080 | bytes 1048576 | tf_op jit(solution)/shard_map/neg | solution.py:35
  8.2 4.5 %convert_element_type.28 = f32[16,65536]{1,0:T(8,128)} convert(s32[16,65536]{1,0:T(8,128)} %param.1) | non-fusion elementwise | flops 1048576 | bytes 8388608 | tf_op jit(solution)/shard_map/convert_element_type | solution.py:65
  12.6 0.7 multiply_reduce_fusion
  14.0 6.6 %copy.16 = f32[2,8,128,512]{3,2,1,0:T(8,128)} copy(f32[2,8,128,512]{3,1,2,0:T(8,128)} %bitcast.33) | data formatting | bytes 8388608
  20.7 0.0 collective-permute-done
  20.7 0.1 reshape.65
  20.8 15.9 %multiply_convert_fusion = bf16[512,16,128]{2,0,1:T(8,128)(2,1)} fusion(f32[]{:T(128)S(6)} %div.61, f32[16,128,512]{2,1,0:T(8,128)} %bitcast.40, f32[16,3,512]{2,1,0:T(4,128)S(1)} %reshape.65, f32[512]{0:T(512)S(1)} %get-tuple-element.5, f32[512]{0:T(512)S(1)} %get-tuple-element.6, f32[512]{0:T(512)S(1)} %get-tuple-element.7, f32[512]{0:T(512)S(1)} %get-tuple-element.4, ...), kind=kOutput, calls=%fused_computation.18 | convolution fusion | flops 6455296000 | bytes 7446532 | tf_op jit(solution)/shard_map/ifn,nk->kif/dot_general | solution.py:49
  36.6 2.9 %copy.9 = bf16[2,256,16,128]{1,3,0,2:T(8,128)(2,1)S(1)} copy(bf16[2,256,16,128]{3,1,0,2:T(8,128)(2,1)} %bitcast.41) | data formatting | bytes 4194304 | tf_op jit(solution)/shard_map/convert_element_type | solution.py:53
  39.5 3.1 %copy.10 = bf16[256,16,256]{2,1,0:T(8,128)(2,1)} copy(bf16[256,16,256]{0,2,1:T(8,128)(2,1)S(1)} %bitcast.37) | data formatting | bytes 4194304 | tf_op jit(solution)/shard_map/convert_element_type | solution.py:53
  42.6 68.0 %all_to_all.33 = bf16[256,16,256]{2,1,0:T(8,128)(2,1)S(1)} all-to-all(bf16[256,16,256]{2,1,0:T(8,128)(2,1)} %copy.10), channel_id=1, replica_groups=mesh['chan'=64,'blk'=4] {'chan'}, dimensions={0} | all-to-all | bytes 4194304 | tf_op jit(solution)/shard_map/all_to_all | solution.py:73
  110.6 0.2 copy.11
  110.8 26.2 %all_to_all.34 = bf16[4,1024,256]{2,1,0:T(8,128)(2,1)S(1)} all-to-all(bf16[4,1024,256]{2,1,0:T(8,128)(2,1)S(1)} %bitcast.39), channel_id=1, replica_groups=mesh['chan'=64,'blk'=4] {'blk'}, dimensions={0} | all-to-all | bytes 4194304 | tf_op jit(solution)/shard_map/all_to_all | solution.py:72
  137.0 2.4 %copy.15 = bf16[1,1024,4,256]{1,3,2,0:T(8,128)(2,1)} copy(bf16[1,1024,4,256]{3,1,2,0:T(8,128)(2,1)S(1)} %bitcast.34) | data formatting | bytes 4194304 | tf_op jit(solution)/shard_map/reshape | solution.py:79
  139.3 0.0 copy-start
  139.3 1.8 %fusion.60 = (bf16[1,1024,4,1,128]{1,4,3,2,0:T(8,128)(2,1)S(1)}, bf16[1,1024,4,1,128]{1,4,3,2,0:T(8,128)(2,1)S(1)}) fusion(bf16[1,1024,4,2,128]{1,4,3,2,0:T(8,128)(2,1)} %bitcast.35), kind=kLoop, calls=%fused_computation.80 | loop fusion | flops 524288 | bytes 4194304 | tf_op jit(solution)/shard_map/slice | solution.py:80
  141.2 0.2 pad_maximum_fusion.1
  141.4 0.2 copy-done
  141.6 4.4 %multiply_bitcast_fusion = f32[1,1024,1024]{2,1,0:T(8,128)} fusion(bf16[1024,1024]{0,1:T(8,128)(2,1)S(1)} %bitcast.42, bf16[1024,1024]{0,1:T(8,128)(2,1)S(1)} %bitcast.36), kind=kOutput, calls=%fused_computation.17 | convolution fusion | flops 2148532224 | bytes 8388608 | tf_op jit(solution)/shard_map/cim,cjm->cij/dot_general | solution.py:88
  146.0 4.4 %fusion.13 = f32[1,1024,1024]{2,1,0:T(8,128)} fusion(bf16[4,1024,256]{2,1,0:T(8,128)(2,1)S(1)} %all_to_all.34), kind=kOutput, calls=%fused_computation.16 | convolution fusion | flops 2148532224 | bytes 6291456 | tf_op jit(solution)/shard_map/cim,cjm->cij/dot_general | solution.py:84
  (1 shorter events, 0.0 us)
Async XLA Ops:
  1.5 19.2 %collective-permute-start = (bf16[16,1536]{1,0:T(8,128)(2,1)S(1)}, bf16[16,1536]{1,0:T(8,128)(2,1)S(1)}, u32[]{:S(2)}, u32[]{:S(2)}) collective-permute-start(bf16[16,1536]{1,0:T(8,128)(2,1)S(1)} %slice_convert_fusion), channel_id=1, source_target_pairs={{0,1},{1,2},{2,3},{4,5},{5,6},{6,7},{8,9},{9,10},{10,11},{12,13},{... | collective-permute-start | bytes 147464 | tf_op jit(solution)/shard_map/ppermute | solution.py:15
  139.3 2.2 %copy-start = (bf16[1,1024,4,256]{1,3,2,0:T(8,128)(2,1)S(1)}, bf16[1,1024,4,256]{1,3,2,0:T(8,128)(2,1)}, u32[]{:S(2)}) copy-start(bf16[1,1024,4,256]{1,3,2,0:T(8,128)(2,1)} %copy.15) | copy-start | bytes 6291460
where the time goes:
time: 151 us; the launch traced here: 150 us
  blocking collectives  94.2 us (62%)
  matrix products  24.7 us (16%)
  local copies, waits for them, and re-layouts  15.4 us (10%)
  other arithmetic  10.2 us (7%)
  starting transfers between devices  4.49 us (3%)
    all_to_all x1, blocking collectives, local(): lax.all_to_all(spectra, 'chan', split_axis=0, concat_axis=1, tiled=True)  68 us
    all_to_all x1, blocking collectives, local(): lax.all_to_all(lax.all_to_all(spectra, 'chan', split_axis=0, concat_axis=...  26.2 us
    dot_general x1, matrix products, to_spectra(): jnp.einsum('ifn,nk->kif', filtered, transform, precision=lax.Precision.HI...  15.9 us
    unnamed x3, local copies, waits for them, and re-layouts  6.82 us
    convert_element_type x2, local copies, waits for them, and re-layouts, to_spectra(): return spectra.reshape(NC, inputs_here, 2 * frames_dev).astype(jnp.bfloat16)  5.92 us
    ppermute x1, starting transfers between devices, shifted(): lax.ppermute(value, axis, [(source, source + steps) for source in range(l...  4.49 us
    convert_element_type x1, other arithmetic, local(): samples = voltages.astype(jnp.float32).reshape(inputs_here, frames_dev, FFT)  4.47 us
    dot_general x1, matrix products, local(): jnp.einsum('cim,cjm->cij', swapped, turned, preferred_element_type=jnp.fl...  4.44 us
  transfers between devices with their start and end apart: 1, of which 0 were waited for; matrix products, arithmetic and copies ran while one was open for 9% of the time, Pallas kernels for 0%

commit v1 on v0

v1 whole, which is shorter than its diff:
```python
import functools

import jax
import jax.numpy as jnp
import numpy as np
from jax import lax
from jax.experimental import pallas as pl
from jax.experimental.pallas import tpu as pltpu
from jax.sharding import PartitionSpec as P

NI = 1024
NC = 256
TAPS = 4
FFT = 512
HALF = FFT // 2
HISTORY = TAPS - 1
MESH = pl.DeviceIdType.MESH


def shifted(value, axis, steps):
    count = lax.axis_size(axis)
    leading, last = (max(0, -steps), min(count, count - steps))
    return lax.ppermute(value, axis, [(source, source + steps) for source in range(leading, last)])


def tables():
    length = TAPS * FFT
    points = np.arange(length, dtype=np.float64)
    window = 0.54 - 0.46 * np.cos(2.0 * np.pi * points / (length - 1))
    taps = (np.sinc((points - (length - 1) / 2.0) / FFT) * window).reshape(TAPS, FFT)
    scale = 1.0 / (56.0 * np.sqrt(FFT * np.mean(np.sum(taps * taps, axis=0))))
    weights = []
    for parity in range(2):
        channel = np.arange(parity, NC, 2)[:, None]
        angle = (channel * np.arange(HALF)[None, :] % FFT) * (2.0 * np.pi / FFT)
        matrix = (scale * np.concatenate([np.cos(angle), -np.sin(angle)], axis=0)).astype(np.float32)
        high = matrix.astype(jnp.bfloat16)
        low = (matrix - high.astype(np.float32)).astype(jnp.bfloat16)
        weights.append(np.concatenate([high, high, low], axis=1))
    return taps.astype(np.float32), np.stack(weights)


def exchange_kernel(frames, v_hbm, halo_hbm, taps_ref, w_ref, x_ref, vb, fold, turn, spec, in_sem, send_sem, recv_sem):
    inputs = v_hbm.shape[0]
    chan = lax.axis_index("chan")
    blk = lax.axis_index("blk")
    chunks = in_sem.shape[0] - 1
    per = frames // chunks
    lead = HISTORY * FFT
    loads = [pltpu.make_async_copy(halo_hbm, vb.at[:, pl.ds(0, lead)], in_sem.at[chunks])]
    for c in range(chunks):
        span = per * FFT
        loads.append(
            pltpu.make_async_copy(
                v_hbm.at[:, pl.ds(c * span, span)], vb.at[:, pl.ds(lead + c * span, span)], in_sem.at[c]
            )
        )
    for load in loads:
        load.start()

    z = chan & 7
    y = (chan >> 4) & 3
    x = ((chan >> 3) & 1) * 2 + (blk >> 1)
    core = blk & 1

    def place(dx, dy, dz, dc):
        tx = (x + dx) & 3
        tc = (((y + dy) & 3) << 4) | ((tx >> 1) << 3) | ((z + dz) & 7)
        tb = ((tx & 1) << 1) | (core ^ dc)
        return tc, tb

    barrier = pltpu.get_barrier_semaphore()

    def greet(r, _):
        for dz in range(8):
            tc, tb = place(r & 3, (r >> 2) & 3, dz, r >> 4)

            def signal():
                pl.semaphore_signal(barrier, inc=1, device_id=(tc, tb), device_id_type=MESH)

            if dz:
                signal()
            else:
                pl.when(r > 0)(signal)
        return 0

    lax.fori_loop(0, 32, greet, 0)

    taps = [taps_ref[pl.ds(t, 1), :] for t in range(TAPS)]

    def sample(f):
        return vb[:, pl.ds(pl.multiple_of(f * FFT, FFT), FFT)].astype(jnp.float32)

    def filter_frames(g, window):
        window = list(window)
        for u in range(4):
            f = g * 4 + u
            window.append(sample(f + HISTORY))
            value = taps[0] * window[0]
            for t in range(1, TAPS):
                value = value + taps[t] * window[t]
            window = window[1:]
            folded = (value[:, :HALF] + value[:, HALF:], value[:, :HALF] - value[:, HALF:])
            for parity in range(2):
                for lane in range(HALF // 128):
                    fold[parity * 2 + lane, pl.ds(f, inputs, stride=frames), :] = folded[parity][
                        :, lane * 128 : (lane + 1) * 128
                    ]
        return tuple(window)

    loads[0].wait()
    window = tuple(sample(f) for f in range(HISTORY))
    for c in range(chunks):
        loads[c + 1].wait()
        window = lax.fori_loop(c * per // 4, (c + 1) * per // 4, filter_frames, window)

    pair = 2 * frames

    def transform(p, _):
        rows = pl.ds(pl.multiple_of(p * pair, pair), pair)
        for parity in range(2):
            value = jnp.concatenate([fold[parity * 2, rows, :], fold[parity * 2 + 1, rows, :]], axis=1)
            high = value.astype(jnp.bfloat16)
            low = (value - high.astype(jnp.float32)).astype(jnp.bfloat16)
            out = lax.dot_general(
                w_ref[parity],
                jnp.concatenate([high, low, high], axis=1),
                (((1,), (1,)), ((), ())),
                preferred_element_type=jnp.float32,
            )
            for h in range(2):
                for part in range(2):
                    start = parity * 2 * inputs + part * inputs + p * 2 + h
                    turn[pl.ds(start, NC // 2, stride=4 * inputs), :] = out[
                        part * NC // 2 : (part + 1) * NC // 2, h * frames : (h + 1) * frames
                    ]
        return 0

    lax.fori_loop(0, inputs // 2, transform, 0)

    def pack(g, _):
        for u in range(8):
            k = g * 8 + u
            both = turn[pl.ds(pl.multiple_of(k * 2 * inputs, 2 * inputs), 2 * inputs), :].astype(jnp.bfloat16)
            spec[k, :, 0:frames] = both[0:inputs]
            spec[k, :, frames : 2 * frames] = both[inputs : 2 * inputs]
        return 0

    lax.fori_loop(0, NC // 8, pack, 0)

    pl.semaphore_wait(barrier, 255)
    row = pl.ds(pl.multiple_of(chan * inputs, inputs), inputs)
    col = pl.ds(pl.multiple_of(blk * pair, pair), pair)
    pltpu.make_async_copy(spec.at[chan * 4 + blk], x_ref.at[row, col], recv_sem).start()

    def send(r, _):
        for dz in range(8):
            tc, tb = place(r & 3, (r >> 2) & 3, dz, r >> 4)

            def copy():
                pltpu.make_async_remote_copy(
                    src_ref=spec.at[tc * 4 + tb],
                    dst_ref=x_ref.at[row, col],
                    send_sem=send_sem,
                    recv_sem=recv_sem,
                    device_id=(tc, tb),
                    device_id_type=MESH,
                ).start()

            if dz:
                copy()
            else:
                pl.when(r > 0)(copy)
        return 0

    lax.fori_loop(0, 32, send, 0)
    pltpu.make_async_copy(spec.at[pl.ds(0, NC - 1)], spec.at[pl.ds(0, NC - 1)], send_sem).wait()
    pltpu.make_async_copy(x_ref, x_ref, recv_sem).wait()


def exchange(voltages, halo, taps, weights):
    inputs, samples = voltages.shape
    frames = samples // FFT
    chunks = 4
    hbm = pl.BlockSpec(memory_space=pl.ANY)
    vmem = pl.BlockSpec(memory_space=pltpu.VMEM)
    return pl.pallas_call(
        functools.partial(exchange_kernel, frames),
        out_shape=jax.ShapeDtypeStruct((NI, 8 * frames), jnp.bfloat16),
        in_specs=[hbm, hbm, vmem, vmem],
        out_specs=hbm,
        scratch_shapes=[
            pltpu.VMEM((inputs, HISTORY * FFT + samples), jnp.int32),
            pltpu.VMEM((FFT // 128, inputs * frames, 128), jnp.float32),
            pltpu.VMEM((NC * 2 * inputs, frames), jnp.float32),
            pltpu.VMEM((NC, inputs, 2 * frames), jnp.bfloat16),
            pltpu.SemaphoreType.DMA((chunks + 1,)),
            pltpu.SemaphoreType.DMA,
            pltpu.SemaphoreType.DMA,
        ],
        compiler_params=pltpu.CompilerParams(
            collective_id=0, has_side_effects=True, vmem_limit_bytes=40 * 1024 * 1024
        ),
        name="filterbank_exchange",
    )(voltages, halo, taps, weights)


def correlate_kernel(frames, total, a_ref, x_ref, re_ref, im_ref):
    left = a_ref[...]
    pieces = []
    for block in range(left.shape[1] // (2 * frames)):
        start = block * 2 * frames
        pieces.append(left[:, start + frames : start + 2 * frames])
        pieces.append(-left[:, start : start + frames])
    swapped = jnp.concatenate(pieces, axis=1)
    contract = (((1,), (1,)), ((), ()))
    right = x_ref[...]
    scale = 1.0 / total
    re_ref[0] = lax.dot_general(left, right, contract, preferred_element_type=jnp.float32) * scale
    im_ref[0] = lax.dot_general(swapped, right, contract, preferred_element_type=jnp.float32) * scale


def correlate(turned, frames):
    rows, depth = turned.shape
    step = 128
    shape = jax.ShapeDtypeStruct((1, rows, rows), jnp.float32)
    out = pl.BlockSpec((1, step, rows), lambda i: (0, i, 0))
    return pl.pallas_call(
        functools.partial(correlate_kernel, frames, depth // 2),
        out_shape=(shape, shape),
        grid=(rows // step,),
        in_specs=[
            pl.BlockSpec((step, depth), lambda i: (i, 0)),
            pl.BlockSpec((rows, depth), lambda i: (0, 0), pipeline_mode=pl.Buffered(1)),
        ],
        out_specs=(out, out),
        compiler_params=pltpu.CompilerParams(vmem_limit_bytes=40 * 1024 * 1024),
        name="correlate",
    )(turned, turned)


def local(voltages):
    frames = voltages.shape[1] // FFT
    taps, weights = tables()
    tail = voltages[:, (frames - HISTORY) * FFT :]
    halo = shifted(tail, "blk", 1)
    turned = exchange(voltages, halo, jnp.asarray(taps), jnp.asarray(weights))
    return correlate(turned, frames)


def solution(mesh):
    return jax.shard_map(
        local,
        mesh=mesh,
        in_specs=(P("chan", "blk"),),
        out_specs=(P(("chan", "blk"), None, None), P(("chan", "blk"), None, None)),
        check_vma=False,
    )
```

time: 151 us -> 92.2 us (0.61)
  blocking collectives: 94.2 us -> 0 us
  Pallas kernels: 0 us -> 79.8 us
  matrix products: 24.7 us -> 0 us
  local copies, waits for them, and re-layouts: 15.4 us -> 4.92 us
  other arithmetic: 10.2 us -> 0 us
  waiting for transfers between devices: 0.01 us -> 1.62 us
    all_to_all x2 -> x0, blocking collectives: 94.2 us -> none  [the longest x1 68 us: local(): lax.all_to_all(spectra, 'chan', split_axis=0, concat_axis=1, tiled=True)]
    pallas_call x0 -> x2, Pallas kernels: none -> 79.8 us  [the longest x1 66.9 us: exchange(): pl.pallas_call(functools.partial(exchange_kernel, frames), out_shape=jax....]
    dot_general x3 -> x0, matrix products: 24.7 us -> none  [the longest x1 15.9 us: to_spectra(): jnp.einsum('ifn,nk->kif', filtered, transform, precision=lax.Precision.HI...]
    convert_element_type x2 -> x0, local copies, waits for them, and re-layouts: 5.92 us -> none  [to_spectra(): return spectra.reshape(NC, inputs_here, 2 * frames_dev).astype(jnp.bfloat16)]
    convert_element_type x1 -> x0, other arithmetic: 4.47 us -> none  [local(): samples = voltages.astype(jnp.float32).reshape(inputs_here, frames_dev, FFT)]
    unnamed x3 -> x6, local copies, waits for them, and re-layouts: 6.82 us -> 4.02 us
    reshape x2 -> x0, local copies, waits for them, and re-layouts: 2.45 us -> none  [the longest x1 2.36 us: local(): stacked = turned.reshape(chan_local, NI, blk_count, 2, frames_dev)]
    neg x1 -> x0, other arithmetic: 2.07 us -> none  [build_transform(): return jnp.concatenate([jnp.cos(angle), -jnp.sin(angle)], axis=1)]
  transfers between devices with their start and end apart: 1 -> 1, of which waited for: 0 -> 1; matrix products, arithmetic and copies ran while one was open for 9% -> 0% of each run, Pallas kernels for 0% -> 0%
where the time goes in v1:
time: 92.2 us; the launch traced here: 91.5 us
  Pallas kernels  79.8 us (87%)
  local copies, waits for them, and re-layouts  4.92 us (5%)
  starting transfers between devices  4.49 us (5%)
  waiting for transfers between devices  1.62 us (2%)
    pallas_call x1, Pallas kernels, exchange(): pl.pallas_call(functools.partial(exchange_kernel, frames), out_shape=jax....  66.9 us
    pallas_call x1, Pallas kernels, correlate(): pl.pallas_call(functools.partial(correlate_kernel, frames, depth // 2), o...  12.9 us
    ppermute x1, starting transfers between devices, shifted(): lax.ppermute(value, axis, [(source, source + steps) for source in range(l...  4.49 us
    unnamed x6, local copies, waits for them, and re-layouts  4.02 us
  transfers between devices with their start and end apart: 1, of which 1 were waited for; matrix products, arithmetic and copies ran while one was open for 0% of the time, Pallas kernels for 0%

profile of v1, /device:TPU:1, one launch (start us, length us, event | category | flops | bytes accessed | tf_op | source)
XLA Modules:
  0.0 91.5 jit_solution(15545341462705796533)
XLA Ops:
  0.6 0.9 slice.3
  1.5 4.5 %collective-permute-start = (s32[16,1536]{1,0:T(8,128)S(1)}, s32[16,1536]{1,0:T(8,128)S(1)}, u32[]{:S(2)}, u32[]{:S(2)}) collective-permute-start(s32[16,1536]{1,0:T(8,128)S(1)} %slice.3), channel_id=1, source_target_pairs={{0,1},{1,2},{2,3},{4,5},{5,6},{6,7},{8,9},{9,10},{10,11},{12,13},{... | collective-permute-start | bytes 294920 | tf_op jit(solution)/shard_map/ppermute | solution.py:23
  6.0 1.6 %collective-permute-done.halo_hbm = s32[16,1536]{1,0:T(8,128)S(1)} collective-permute-done((s32[16,1536]{1,0:T(8,128)S(1)}, s32[16,1536]{1,0:T(8,128)S(1)}, u32[]{:S(2)}, u32[]{:S(2)}) %collective-permute-start) | collective-permute-done | bytes 98336 | tf_op jit(solution)/shard_map/ppermute | solution.py:23
  7.6 0.0 copy-start
  7.6 2.2 %copy-done = s32[16,65536]{1,0:T(8,128)S(1)} copy-done((s32[16,65536]{1,0:T(8,128)S(1)}, s32[16,65536]{1,0:T(8,128)}, u32[]{:S(2)}) %copy-start) | copy-done | bytes 4194328
  9.8 0.0 copy-start.1
  9.8 1.1 %copy-done.1 = bf16[2,256,768]{2,1,0:T(8,128)(2,1)S(1)} copy-done((bf16[2,256,768]{2,1,0:T(8,128)(2,1)S(1)}, bf16[2,256,768]{2,1,0:T(8,128)(2,1)}, u32[]{:S(2)}) %copy-start.1) | copy-done | bytes 786456
  11.0 0.0 copy-start.2
  11.0 0.7 copy-done.2
  11.7 66.9 %filterbank_exchange.1.a_ref.x_ref = bf16[1024,1024]{1,0:T(8,128)(2,1)S(1)} custom-call(s32[16,65536]{1,0:T(8,128)S(1)} %copy-done, s32[16,1536]{1,0:T(8,128)S(1)} %collective-permute-done.halo_hbm, f32[4,512]{1,0:T(4,128)S(1)} %copy-done.2, bf16[2,256,768]{2,1,0:T(8,128)(2,1)S(1)} %copy-done.1), custom_call_target="tpu_custom_call" | custom-call | tf_op jit(solution)/shard_map/filterbank_exchange/pallas_call | solution.py:187
  78.6 12.9 %correlate.1 = (f32[1,1024,1024]{2,1,0:T(8,128)}, f32[1,1024,1024]{2,1,0:T(8,128)}) custom-call(bf16[1024,1024]{1,0:T(8,128)(2,1)S(1)} %filterbank_exchange.1.a_ref.x_ref, bf16[1024,1024]{1,0:T(8,128)(2,1)S(1)} %filterbank_exchange.1.a_ref.x_ref), custom_call_target="tpu_custom_call" | custom-call | tf_op jit(solution)/shard_map/correlate/pallas_call | solution.py:228
Async XLA Ops:
  1.5 6.1 %collective-permute-start = (s32[16,1536]{1,0:T(8,128)S(1)}, s32[16,1536]{1,0:T(8,128)S(1)}, u32[]{:S(2)}, u32[]{:S(2)}) collective-permute-start(s32[16,1536]{1,0:T(8,128)S(1)} %slice.3), channel_id=1, source_target_pairs={{0,1},{1,2},{2,3},{4,5},{5,6},{6,7},{8,9},{9,10},{10,11},{12,13},{... | collective-permute-start | bytes 294920 | tf_op jit(solution)/shard_map/ppermute | solution.py:23
  7.6 2.2 %copy-start = (s32[16,65536]{1,0:T(8,128)S(1)}, s32[16,65536]{1,0:T(8,128)}, u32[]{:S(2)}) copy-start(s32[16,65536]{1,0:T(8,128)} %v_hbm.1) | copy-start | bytes 12582916
  9.8 1.1 %copy-start.1 = (bf16[2,256,768]{2,1,0:T(8,128)(2,1)S(1)}, bf16[2,256,768]{2,1,0:T(8,128)(2,1)}, u32[]{:S(2)}) copy-start(bf16[2,256,768]{2,1,0:T(8,128)(2,1)} %constant.5.clone.w_ref) | copy-start | bytes 2359300
  11.0 0.7 copy-start.2

commit v2 on v1

v2 whole, which is shorter than its diff:
```python
import functools

import jax
import jax.numpy as jnp
import numpy as np
from jax import lax
from jax.experimental import pallas as pl
from jax.experimental.pallas import tpu as pltpu
from jax.sharding import PartitionSpec as P

NI = 1024
NC = 256
TAPS = 4
FFT = 512
HALF = FFT // 2
HISTORY = TAPS - 1
MESH = pl.DeviceIdType.MESH


def shifted(value, axis, steps):
    count = lax.axis_size(axis)
    leading, last = (max(0, -steps), min(count, count - steps))
    return lax.ppermute(value, axis, [(source, source + steps) for source in range(leading, last)])


def tables():
    length = TAPS * FFT
    points = np.arange(length, dtype=np.float64)
    window = 0.54 - 0.46 * np.cos(2.0 * np.pi * points / (length - 1))
    taps = (np.sinc((points - (length - 1) / 2.0) / FFT) * window).reshape(TAPS, FFT)
    scale = 1.0 / (56.0 * np.sqrt(FFT * np.mean(np.sum(taps * taps, axis=0))))
    weights = []
    for parity in range(2):
        channel = np.arange(parity, NC, 2)[:, None]
        angle = (channel * np.arange(HALF)[None, :] % FFT) * (2.0 * np.pi / FFT)
        matrix = (scale * np.concatenate([np.cos(angle), -np.sin(angle)], axis=0)).astype(np.float32)
        high = matrix.astype(jnp.bfloat16)
        low = (matrix - high.astype(np.float32)).astype(jnp.bfloat16)
        weights.append(np.concatenate([high, high, low], axis=1))
    return taps.astype(np.float32), np.stack(weights)


FOLD_PITCH = 132
TURN_PITCH = 36


def exchange_kernel(
    frames,
    v_hbm,
    halo_hbm,
    taps_hbm,
    w_hbm,
    last_ref,
    re_ref,
    im_ref,
    vb,
    taps_ref,
    w_ref,
    fold,
    turn,
    spec,
    landed,
    in_sem,
    send_sem,
    recv_sem,
):
    inputs = v_hbm.shape[0]
    chan = lax.axis_index("chan")
    blk = lax.axis_index("blk")
    chunks = in_sem.shape[0] - 3
    per = frames // chunks
    lead = HISTORY * FFT
    table_loads = [
        pltpu.make_async_copy(taps_hbm, taps_ref, in_sem.at[chunks + 1]),
        pltpu.make_async_copy(w_hbm, w_ref, in_sem.at[chunks + 2]),
    ]
    loads = [pltpu.make_async_copy(halo_hbm, vb.at[:, pl.ds(0, lead)], in_sem.at[chunks])]
    for c in range(chunks):
        span = per * FFT
        loads.append(
            pltpu.make_async_copy(
                v_hbm.at[:, pl.ds(c * span, span)], vb.at[:, pl.ds(lead + c * span, span)], in_sem.at[c]
            )
        )
    for load in (table_loads[0], *loads, table_loads[1]):
        load.start()

    z = chan & 7
    y = (chan >> 4) & 3
    x = ((chan >> 3) & 1) * 2 + (blk >> 1)
    core = blk & 1

    def place(dx, dy, dz, dc):
        tx = (x + dx) & 3
        tc = (((y + dy) & 3) << 4) | ((tx >> 1) << 3) | ((z + dz) & 7)
        tb = ((tx & 1) << 1) | (core ^ dc)
        return tc, tb

    barrier = pltpu.get_barrier_semaphore()

    def greet(r, _):
        for dz in (4, 3, 5, 2, 6, 1, 7, 0):
            tc, tb = place((r & 3) ^ 2, ((r >> 2) & 3) ^ 2, dz, r >> 4)

            def signal():
                pl.semaphore_signal(barrier, inc=1, device_id=(tc, tb), device_id_type=MESH)

            if dz:
                signal()
            else:
                pl.when(r != 10)(signal)
        return 0

    lax.fori_loop(0, 32, greet, 0)

    def sample(f):
        return vb[:, pl.ds(pl.multiple_of(f * FFT, FFT), FFT)].astype(jnp.float32)

    table_loads[0].wait()
    taps = [taps_ref[pl.ds(t, 1), :] for t in range(TAPS)]

    def filter_frames(g, window):
        window = list(window)
        for u in range(4):
            f = g * 4 + u
            window.append(sample(f + HISTORY))
            value = taps[0] * window[0]
            for t in range(1, TAPS):
                value = value + taps[t] * window[t]
            window = window[1:]
            folded = (value[:, :HALF] + value[:, HALF:], value[:, :HALF] - value[:, HALF:])
            for parity in range(2):
                for lane in range(HALF // 128):
                    fold[parity * 2 + lane, pl.ds(f, inputs, stride=FOLD_PITCH), :] = folded[parity][
                        :, lane * 128 : (lane + 1) * 128
                    ]
        return tuple(window)

    loads[0].wait()
    window = tuple(sample(f) for f in range(HISTORY))
    for c in range(chunks):
        loads[c + 1].wait()
        window = lax.fori_loop(c * per // 4, (c + 1) * per // 4, filter_frames, window)

    def transform(slot, parity):
        def body(p, _):
            base = pl.multiple_of(p * 2 * FOLD_PITCH, 8)
            halves = []
            for lane in range(HALF // 128):
                source = fold.at[parity * 2 + lane]
                halves.append(
                    jnp.concatenate(
                        [source[pl.ds(base, frames), :], source[pl.ds(base + FOLD_PITCH, frames), :]], axis=0
                    )
                )
            value = jnp.concatenate(halves, axis=1)
            high = value.astype(jnp.bfloat16)
            low = (value - high.astype(jnp.float32)).astype(jnp.bfloat16)
            out = lax.dot_general(
                w_ref[parity],
                jnp.concatenate([high, low, high], axis=1),
                (((1,), (1,)), ((), ())),
                preferred_element_type=jnp.float32,
            )
            for h in range(2):
                for part in range(2):
                    turn[slot, pl.ds(part * inputs + p * 2 + h, NC // 2, stride=TURN_PITCH), :] = out[
                        part * NC // 2 : (part + 1) * NC // 2, h * frames : (h + 1) * frames
                    ]
            return 0

        lax.fori_loop(0, inputs // 2, body, 0)

    def pack(phase, slot, half):
        def body(g, _):
            for u in range(4):
                m = g * 4 + u
                start = (2 * m + half) * TURN_PITCH
                for part in range(2):
                    spec[phase, m, :, part * frames : (part + 1) * frames] = turn[
                        slot, pl.ds(start + part * inputs, inputs), :
                    ].astype(jnp.bfloat16)
            return 0

        lax.fori_loop(0, NC // 16, body, 0)

    row = pl.ds(pl.multiple_of(chan * inputs, inputs), inputs)

    def landing(phase):
        return last_ref if phase == 3 else landed.at[phase]

    def send(phase):
        shift_x, shift_core = phase & 1, phase >> 1
        if phase == 0:
            pltpu.make_async_copy(spec.at[0, chan], landing(0).at[row, :], recv_sem.at[0]).start()

        def body(r, _):
            for dz in (1, 7, 2, 6, 3, 5, 4, 0):
                tc, tb = place(shift_x + 2 * (r & 1), r >> 1, dz, shift_core)

                def copy():
                    pltpu.make_async_remote_copy(
                        src_ref=spec.at[phase, tc],
                        dst_ref=landing(phase).at[row, :],
                        send_sem=send_sem,
                        recv_sem=recv_sem.at[phase],
                        device_id=(tc, tb),
                        device_id_type=MESH,
                    ).start()

                if dz or phase:
                    copy()
                else:
                    pl.when(r > 0)(copy)
            return 0

        lax.fori_loop(0, 8, body, 0)

    table_loads[1].wait()
    for group in range(2):
        parity = core ^ group
        transform(group, parity)
        for shift_x in range(2):
            phase = group * 2 + shift_x
            pack(phase, group, (blk >> 1) ^ shift_x)
            if phase == 0:
                pl.semaphore_wait(barrier, 255)
            send(phase)

    def accumulate(phase):
        source = landed.at[phase]
        step = 256

        def body(r, _):
            rows = pl.ds(pl.multiple_of(r * step, step), step)
            left = source[rows, :]
            swapped = jnp.concatenate([left[:, frames:], -left[:, :frames]], axis=1)
            for operand, out in ((left, re_ref), (swapped, im_ref)):
                value = lax.dot_general(
                    operand, source[...], (((1,), (1,)), ((), ())), preferred_element_type=jnp.float32
                )
                if phase == 0:
                    out[rows, :] = value
                else:
                    out[rows, :] += value
            return 0

        lax.fori_loop(0, NI // step, body, 0)

    for phase in range(4):
        block = landing(phase)
        pltpu.make_async_copy(block, block, recv_sem.at[phase]).wait()
        if phase < 3:
            accumulate(phase)
    pltpu.make_async_copy(landed, landed, send_sem).wait()
    sent = spec.at[0, pl.ds(0, NC // 4 - 1)]
    pltpu.make_async_copy(sent, sent, send_sem).wait()


def exchange(voltages, halo, taps, weights):
    inputs, samples = voltages.shape
    frames = samples // FFT
    chunks = 4
    hbm = pl.BlockSpec(memory_space=pltpu.HBM)
    vmem = pl.BlockSpec(memory_space=pltpu.VMEM)
    square = jax.ShapeDtypeStruct((NI, NI), jnp.float32)
    return pl.pallas_call(
        functools.partial(exchange_kernel, frames),
        out_shape=(jax.ShapeDtypeStruct((NI, 2 * frames), jnp.bfloat16), square, square),
        in_specs=[hbm, hbm, hbm, hbm],
        out_specs=(vmem, vmem, vmem),
        scratch_shapes=[
            pltpu.VMEM((inputs, HISTORY * FFT + samples), jnp.int32),
            pltpu.VMEM(taps.shape, taps.dtype),
            pltpu.VMEM(weights.shape, weights.dtype),
            pltpu.VMEM((FFT // 128, inputs * FOLD_PITCH, 128), jnp.float32),
            pltpu.VMEM((2, NC // 2 * TURN_PITCH, frames), jnp.float32),
            pltpu.VMEM((4, NC // 4, inputs, 2 * frames), jnp.bfloat16),
            pltpu.VMEM((3, NI, 2 * frames), jnp.bfloat16),
            pltpu.SemaphoreType.DMA((chunks + 3,)),
            pltpu.SemaphoreType.DMA,
            pltpu.SemaphoreType.DMA((4,)),
        ],
        compiler_params=pltpu.CompilerParams(
            collective_id=0, has_side_effects=True, vmem_limit_bytes=44 * 1024 * 1024
        ),
        name="filterbank_exchange",
    )(voltages, halo, taps, weights)


def finish_kernel(frames, total, step, last_ref, re_in, im_in, re_ref, im_ref):
    rows = pl.ds(pl.multiple_of(pl.program_id(0) * step, step), step)
    left = last_ref[rows, :]
    swapped = jnp.concatenate([left[:, frames:], -left[:, :frames]], axis=1)
    for operand, partial, out in ((left, re_in, re_ref), (swapped, im_in, im_ref)):
        value = lax.dot_general(
            operand, last_ref[...], (((1,), (1,)), ((), ())), preferred_element_type=jnp.float32
        )
        out[0] = (partial[rows, :] + value) * (1.0 / total)


def finish(last, real, imag, frames):
    step = 128
    shape = jax.ShapeDtypeStruct((1, NI, NI), jnp.float32)
    out = pl.BlockSpec((1, step, NI), lambda i: (0, i, 0))
    vmem = pl.BlockSpec(memory_space=pltpu.VMEM)
    return pl.pallas_call(
        functools.partial(finish_kernel, frames, 4 * frames, step),
        out_shape=(shape, shape),
        grid=(NI // step,),
        in_specs=[vmem, vmem, vmem],
        out_specs=(out, out),
        compiler_params=pltpu.CompilerParams(vmem_limit_bytes=24 * 1024 * 1024),
        name="finish",
    )(last, real, imag)


def local(voltages):
    frames = voltages.shape[1] // FFT
    taps, weights = tables()
    tail = voltages[:, (frames - HISTORY) * FFT :]
    halo = shifted(tail, "blk", 1)
    last, real, imag = exchange(voltages, halo, jnp.asarray(taps), jnp.asarray(weights))
    return finish(last, real, imag, frames)


def solution(mesh):
    return jax.shard_map(
        local,
        mesh=mesh,
        in_specs=(P("chan", "blk"),),
        out_specs=(P(("chan", "blk"), None, None), P(("chan", "blk"), None, None)),
        check_vma=False,
    )
```

time: 92.2 us -> 76.5 us (0.83)
  Pallas kernels: 79.8 us -> 66.8 us
  local copies, waits for them, and re-layouts: 4.92 us -> 2.73 us
    pallas_call x2, Pallas kernels: 79.8 us -> 66.8 us  [the longest x1 61.1 us: exchange(): pl.pallas_call(functools.partial(exchange_kernel, frames), out_shape=(jax...]
    unnamed x6 -> x4, local copies, waits for them, and re-layouts: 4.02 us -> 1.83 us
where the time goes in v2:
time: 76.5 us; the launch traced here: 76.3 us
  Pallas kernels  66.8 us (87%)
  starting transfers between devices  4.49 us (6%)
  local copies, waits for them, and re-layouts  2.73 us (4%)
  waiting for transfers between devices  1.62 us (2%)
    pallas_call x1, Pallas kernels, exchange(): pl.pallas_call(functools.partial(exchange_kernel, frames), out_shape=(jax...  61.1 us
    pallas_call x1, Pallas kernels, finish(): pl.pallas_call(functools.partial(finish_kernel, frames, 4 * frames, step)...  5.67 us
    ppermute x1, starting transfers between devices, shifted(): lax.ppermute(value, axis, [(source, source + steps) for source in range(l...  4.49 us
    unnamed x4, local copies, waits for them, and re-layouts  1.83 us
    ppermute x1, waiting for transfers between devices, shifted(): lax.ppermute(value, axis, [(source, source + steps) for source in range(l...  1.62 us
  transfers between devices with their start and end apart: 1, of which 1 were waited for; matrix products, arithmetic and copies ran while one was open for 0% of the time, Pallas kernels for 0%

profile of v2, /device:TPU:1, one launch (start us, length us, event | category | flops | bytes accessed | tf_op | source)
XLA Modules:
  0.0 76.3 jit_solution(4860121580826535199)
XLA Ops:
  0.6 0.9 %slice.3 = s32[16,1536]{1,0:T(8,128)S(1)} slice(s32[16,65536]{1,0:T(8,128)} %v_hbm.1), slice={[0:16], [64000:65536]} | slice | bytes 196608 | tf_op jit(solution)/shard_map/slice | solution.py:321
  1.5 4.5 %collective-permute-start = (s32[16,1536]{1,0:T(8,128)S(1)}, s32[16,1536]{1,0:T(8,128)S(1)}, u32[]{:S(2)}, u32[]{:S(2)}) collective-permute-start(s32[16,1536]{1,0:T(8,128)S(1)} %slice.3), channel_id=1, source_target_pairs={{0,1},{1,2},{2,3},{4,5},{5,6},{6,7},{8,9},{9,10},{10,11},{12,13},{... | collective-permute-start | bytes 294920 | tf_op jit(solution)/shard_map/ppermute | solution.py:23
  6.0 1.6 %collective-permute-done.halo_hbm = s32[16,1536]{1,0:T(8,128)S(1)} collective-permute-done((s32[16,1536]{1,0:T(8,128)S(1)}, s32[16,1536]{1,0:T(8,128)S(1)}, u32[]{:S(2)}, u32[]{:S(2)}) %collective-permute-start) | collective-permute-done | bytes 98336 | tf_op jit(solution)/shard_map/ppermute | solution.py:23
  7.6 0.0 copy-start
  7.6 1.1 %copy-done = bf16[2,256,768]{2,1,0:T(8,128)(2,1)S(1)} copy-done((bf16[2,256,768]{2,1,0:T(8,128)(2,1)S(1)}, bf16[2,256,768]{2,1,0:T(8,128)(2,1)}, u32[]{:S(2)}) %copy-start) | copy-done | bytes 786456
  8.8 0.0 copy-start.1
  8.8 0.7 copy-done.1
  9.5 61.1 %filterbank_exchange.1 = (bf16[1024,256]{1,0:T(8,128)(2,1)S(1)}, f32[1024,1024]{1,0:T(8,128)S(1)}, f32[1024,1024]{1,0:T(8,128)S(1)}) custom-call(s32[16,65536]{1,0:T(8,128)} %v_hbm.1, s32[16,1536]{1,0:T(8,128)S(1)} %collective-permute-done.halo_hbm, f32[4,512]{1,0:T(4,128)S(1)} %copy-done.1, bf16[2,256,768]{2,1,0:T(8,128)(2,1)S(1)} %copy-done), custom_call_target="tpu_custom_call" | custom-call | tf_op jit(solution)/shard_map/filterbank_exchange/pallas_call | solution.py:267
  70.6 5.7 %finish.1 = (f32[1,1024,1024]{2,1,0:T(8,128)}, f32[1,1024,1024]{2,1,0:T(8,128)}) custom-call(bf16[1024,256]{1,0:T(8,128)(2,1)S(1)} %get-tuple-element.5.last_ref, f32[1024,1024]{1,0:T(8,128)S(1)} %get-tuple-element.6.re_in, f32[1024,1024]{1,0:T(8,128)S(1)} %get-tuple-element.7.im_in), custom_call_target="tpu_custom_call" | custom-call | tf_op jit(solution)/shard_map/finish/pallas_call | solution.py:307
Async XLA Ops:
  1.5 6.1 %collective-permute-start = (s32[16,1536]{1,0:T(8,128)S(1)}, s32[16,1536]{1,0:T(8,128)S(1)}, u32[]{:S(2)}, u32[]{:S(2)}) collective-permute-start(s32[16,1536]{1,0:T(8,128)S(1)} %slice.3), channel_id=1, source_target_pairs={{0,1},{1,2},{2,3},{4,5},{5,6},{6,7},{8,9},{9,10},{10,11},{12,13},{... | collective-permute-start | bytes 294920 | tf_op jit(solution)/shard_map/ppermute | solution.py:23
  7.6 1.1 %copy-start = (bf16[2,256,768]{2,1,0:T(8,128)(2,1)S(1)}, bf16[2,256,768]{2,1,0:T(8,128)(2,1)}, u32[]{:S(2)}) copy-start(bf16[2,256,768]{2,1,0:T(8,128)(2,1)} %constant.5.clone.w_hbm) | copy-start | bytes 2359300
  8.8 0.7 copy-start.1

commit v3 on v2

v3 whole, which is shorter than its diff:
```python
import functools

import jax
import jax.numpy as jnp
import numpy as np
from jax import lax
from jax.experimental import pallas as pl
from jax.experimental.pallas import tpu as pltpu
from jax.sharding import PartitionSpec as P

NI = 1024
NC = 256
TAPS = 4
FFT = 512
HALF = FFT // 2
HISTORY = TAPS - 1
MESH = pl.DeviceIdType.MESH


def tables():
    length = TAPS * FFT
    points = np.arange(length, dtype=np.float64)
    window = 0.54 - 0.46 * np.cos(2.0 * np.pi * points / (length - 1))
    taps = (np.sinc((points - (length - 1) / 2.0) / FFT) * window).reshape(TAPS, FFT)
    scale = 1.0 / (56.0 * np.sqrt(FFT * np.mean(np.sum(taps * taps, axis=0))))
    weights = []
    for parity in range(2):
        channel = np.arange(parity, NC, 2)[:, None]
        angle = (channel * np.arange(HALF)[None, :] % FFT) * (2.0 * np.pi / FFT)
        weights.append(scale * np.concatenate([np.cos(angle), -np.sin(angle)], axis=0))
    return np.concatenate([*weights, taps.reshape(2 * TAPS, HALF)], axis=0).astype(np.float32)


FOLD_PITCH = 132
TURN_PITCH = 36
EARLY = 2


def exchange_kernel(
    frames,
    v_hbm,
    table_hbm,
    last_ref,
    re_ref,
    im_ref,
    vb,
    table,
    w_ref,
    tail,
    tail_out,
    halo,
    fold,
    head,
    turn,
    extra,
    spec,
    landed,
    in_sem,
    halo_sem,
    send_sem,
    recv_sem,
):
    inputs = v_hbm.shape[0]
    chan = lax.axis_index("chan")
    blk = lax.axis_index("blk")
    blocks = lax.axis_size("blk")
    chunks = in_sem.shape[0] - 2
    per = frames // chunks
    lead = HISTORY * FFT
    table_load = pltpu.make_async_copy(table_hbm, table, in_sem.at[chunks])
    tail_load = pltpu.make_async_copy(v_hbm.at[:, pl.ds(frames * FFT - lead, lead)], tail, in_sem.at[chunks + 1])
    loads = []
    for c in range(chunks):
        span = pl.ds(c * per * FFT, per * FFT)
        loads.append(pltpu.make_async_copy(v_hbm.at[:, span], vb.at[:, span], in_sem.at[c]))
    for load in (table_load, *loads, tail_load):
        load.start()

    z = chan & 7
    y = (chan >> 4) & 3
    x = ((chan >> 3) & 1) * 2 + (blk >> 1)
    core = blk & 1
    along = [(z + dz) & 7 for dz in range(8)]

    def place(dx, dy, dc):
        tx = (x + dx) & 3
        return (((y + dy) & 3) << 4) | ((tx >> 1) << 3), ((tx & 1) << 1) | (core ^ dc)

    barrier = pltpu.get_barrier_semaphore()

    def greet(r, _):
        base, tb = place((r & 3) ^ 2, ((r >> 2) & 3) ^ 2, r >> 4)
        for dz in (4, 3, 5, 2, 6, 1, 7, 0):

            def signal():
                pl.semaphore_signal(barrier, inc=1, device_id=(base | along[dz], tb), device_id_type=MESH)

            if dz:
                signal()
            else:
                pl.when(r != 10)(signal)
        return 0

    lax.fori_loop(0, 32, greet, 0)

    head[...] = jnp.zeros_like(head)
    table_load.wait()
    for parity in range(2):
        value = table[pl.ds(parity * 2 * (NC // 2), NC), :]
        high = value.astype(jnp.bfloat16)
        w_ref[parity, 0:NC, :] = high
        w_ref[parity, NC : 2 * NC, :] = (value - high.astype(jnp.float32)).astype(jnp.bfloat16)

    def tap(t):
        row = 2 * NC + 2 * t
        return jnp.concatenate([table[row : row + 1, :], table[row + 1 : row + 2, :]], axis=1)

    taps = [tap(t) for t in range(TAPS)]

    def place_frame(ref, f, pitch, value):
        folded = (value[:, :HALF] + value[:, HALF:], value[:, :HALF] - value[:, HALF:])
        for parity in range(2):
            for lane in range(HALF // 128):
                ref[parity * 2 + lane, pl.ds(f, inputs, stride=pitch), :] = folded[parity][
                    :, lane * 128 : (lane + 1) * 128
                ]

    def filter_frames(g, window):
        window = list(window)
        for u in range(4):
            f = g * 4 + u
            window.append(vb[:, pl.ds(pl.multiple_of(f * FFT, FFT), FFT)].astype(jnp.float32))
            value = taps[0] * window[0]
            for t in range(1, TAPS):
                value = value + taps[t] * window[t]
            window = window[1:]
            place_frame(fold, f, FOLD_PITCH, value)
        return tuple(window)

    window = tuple(jnp.zeros((inputs, FFT), jnp.float32) for _ in range(HISTORY))
    for c in range(chunks):
        loads[c].wait()
        window = lax.fori_loop(c * per // 4, (c + 1) * per // 4, filter_frames, window)

    def spectra(parity, value):
        high = value.astype(jnp.bfloat16)
        low = (value - high.astype(jnp.float32)).astype(jnp.bfloat16)
        contract = (((1,), (1,)), ((), ()))
        both = lax.dot_general(w_ref[parity], high, contract, preferred_element_type=jnp.float32)
        rest = lax.dot_general(w_ref[parity, 0:NC, :], low, contract, preferred_element_type=jnp.float32)
        return both[0:NC] + (both[NC : 2 * NC] + rest)

    def transform(slot, parity, first, last):
        def body(p, _):
            base = pl.multiple_of(p * 2 * FOLD_PITCH, 8)
            halves = []
            for lane in range(HALF // 128):
                source = fold.at[parity * 2 + lane]
                halves.append(
                    jnp.concatenate(
                        [source[pl.ds(base, frames), :], source[pl.ds(base + FOLD_PITCH, frames), :]], axis=0
                    )
                )
            out = spectra(parity, jnp.concatenate(halves, axis=1))
            for h in range(2):
                for part in range(2):
                    turn[slot, pl.ds(part * inputs + p * 2 + h, NC // 2, stride=TURN_PITCH), :] = out[
                        part * NC // 2 : (part + 1) * NC // 2, h * frames : (h + 1) * frames
                    ]
            return 0

        lax.fori_loop(first, last, body, 0)

    slots = head.shape[1] // inputs

    def patch(parity):
        out = spectra(parity, jnp.concatenate([head[parity * 2], head[parity * 2 + 1]], axis=1))
        for i in range(inputs):
            for part in range(2):
                value = out[part * NC // 2 : (part + 1) * NC // 2, :]
                if i:
                    value = pltpu.roll(value, 128 - slots * i, 1)
                extra[pl.ds(part * inputs + i, NC // 2, stride=TURN_PITCH), :] = value

    first_lanes = lax.broadcasted_iota(jnp.int32, (inputs, frames), 1) < slots

    def pack(phase, slot, half):
        def body(g, _):
            for u in range(4):
                m = g * 4 + u
                start = (2 * m + half) * TURN_PITCH
                for part in range(2):
                    rows = pl.ds(start + part * inputs, inputs)
                    value = turn[slot, rows, :] + jnp.where(first_lanes, extra[rows, :], 0.0)
                    spec[phase, m, :, part * frames : (part + 1) * frames] = value.astype(jnp.bfloat16)
            return 0

        lax.fori_loop(0, NC // 16, body, 0)

    row = pl.ds(pl.multiple_of(chan * inputs, inputs), inputs)

    def landing(phase):
        return last_ref if phase == 3 else landed.at[phase]

    def send(phase):
        shift_x, shift_core = phase & 1, phase >> 1
        if phase == 0:
            pltpu.make_async_copy(spec.at[0, chan], landing(0).at[row, :], recv_sem.at[0]).start()

        def body(r, _):
            base, tb = place(shift_x + 2 * (r & 1), r >> 1, shift_core)
            for dz in (1, 7, 2, 6, 3, 5, 4, 0):
                tc = base | along[dz]

                def copy():
                    pltpu.make_async_remote_copy(
                        src_ref=spec.at[phase, tc],
                        dst_ref=landing(phase).at[row, :],
                        send_sem=send_sem,
                        recv_sem=recv_sem.at[phase],
                        device_id=(tc, tb),
                        device_id_type=MESH,
                    ).start()

                if dz or phase:
                    copy()
                else:
                    pl.when(r > 0)(copy)
            return 0

        lax.fori_loop(0, 8, body, 0)

    tail_load.wait()
    tail_out[...] = tail[...].astype(jnp.bfloat16)
    pairs = inputs // 2
    transform(0, core, 0, pairs // 2)
    pl.semaphore_wait(barrier, 255)
    onward = pltpu.make_async_remote_copy(
        src_ref=tail_out,
        dst_ref=halo,
        send_sem=halo_sem.at[0],
        recv_sem=halo_sem.at[1],
        device_id=(chan, jnp.minimum(blk + 1, blocks - 1)),
        device_id_type=MESH,
    )

    @pl.when(blk < blocks - 1)
    def _():
        onward.start()

    transform(0, core, pairs // 2, pairs)
    transform(1, core ^ 1, 0, EARLY)

    @pl.when(blk > 0)
    def _():
        onward.wait_recv()
        for f in range(HISTORY):
            value = None
            for t in range(HISTORY - f):
                earlier = halo[:, (f + t) * FFT : (f + t + 1) * FFT].astype(jnp.float32)
                value = taps[t] * earlier if value is None else value + taps[t] * earlier
            place_frame(head, f, slots, value)

    for group in range(2):
        if group:
            transform(1, core ^ 1, EARLY, pairs)
        patch(core ^ group)
        for shift_x in range(2):
            phase = group * 2 + shift_x
            pack(phase, group, (blk >> 1) ^ shift_x)
            send(phase)

    @pl.when(blk < blocks - 1)
    def _():
        onward.wait_send()

    def accumulate(phase):
        source = landed.at[phase]
        step = 256

        def body(r, _):
            rows = pl.ds(pl.multiple_of(r * step, step), step)
            left = source[rows, :]
            swapped = jnp.concatenate([left[:, frames:], -left[:, :frames]], axis=1)
            for operand, out in ((left, re_ref), (swapped, im_ref)):
                value = lax.dot_general(
                    operand, source[...], (((1,), (1,)), ((), ())), preferred_element_type=jnp.float32
                )
                if phase == 0:
                    out[rows, :] = value
                else:
                    out[rows, :] += value
            return 0

        lax.fori_loop(0, NI // step, body, 0)

    for phase in range(4):
        block = landing(phase)
        pltpu.make_async_copy(block, block, recv_sem.at[phase]).wait()
        if phase < 3:
            accumulate(phase)
    pltpu.make_async_copy(landed, landed, send_sem).wait()
    sent = spec.at[0, pl.ds(0, NC // 4 - 1)]
    pltpu.make_async_copy(sent, sent, send_sem).wait()


def exchange(voltages, table):
    inputs, samples = voltages.shape
    frames = samples // FFT
    chunks = 4
    hbm = pl.BlockSpec(memory_space=pltpu.HBM)
    vmem = pl.BlockSpec(memory_space=pltpu.VMEM)
    square = jax.ShapeDtypeStruct((NI, NI), jnp.float32)
    return pl.pallas_call(
        functools.partial(exchange_kernel, frames),
        out_shape=(jax.ShapeDtypeStruct((NI, 2 * frames), jnp.bfloat16), square, square),
        in_specs=[hbm, hbm],
        out_specs=(vmem, vmem, vmem),
        scratch_shapes=[
            pltpu.VMEM((inputs, samples), jnp.int32),
            pltpu.VMEM(table.shape, jnp.float32),
            pltpu.VMEM((2, 2 * NC, HALF), jnp.bfloat16),
            pltpu.VMEM((inputs, HISTORY * FFT), jnp.int32),
            pltpu.VMEM((inputs, HISTORY * FFT), jnp.bfloat16),
            pltpu.VMEM((inputs, HISTORY * FFT), jnp.bfloat16),
            pltpu.VMEM((FFT // 128, inputs * FOLD_PITCH, 128), jnp.float32),
            pltpu.VMEM((FFT // 128, 128, 128), jnp.float32),
            pltpu.VMEM((2, NC // 2 * TURN_PITCH, frames), jnp.float32),
            pltpu.VMEM((NC // 2 * TURN_PITCH, frames), jnp.float32),
            pltpu.VMEM((4, NC // 4, inputs, 2 * frames), jnp.bfloat16),
            pltpu.VMEM((3, NI, 2 * frames), jnp.bfloat16),
            pltpu.SemaphoreType.DMA((chunks + 2,)),
            pltpu.SemaphoreType.DMA((2,)),
            pltpu.SemaphoreType.DMA,
            pltpu.SemaphoreType.DMA((4,)),
        ],
        compiler_params=pltpu.CompilerParams(
            collective_id=0, has_side_effects=True, vmem_limit_bytes=44 * 1024 * 1024
        ),
        name="filterbank_exchange",
    )(voltages, table)


def finish_kernel(frames, total, step, last_ref, re_in, im_in, re_ref, im_ref):
    rows = pl.ds(pl.multiple_of(pl.program_id(0) * step, step), step)
    left = last_ref[rows, :]
    swapped = jnp.concatenate([left[:, frames:], -left[:, :frames]], axis=1)
    for operand, partial, out in ((left, re_in, re_ref), (swapped, im_in, im_ref)):
        value = lax.dot_general(
            operand, last_ref[...], (((1,), (1,)), ((), ())), preferred_element_type=jnp.float32
        )
        out[0] = (partial[rows, :] + value) * (1.0 / total)


def finish(last, real, imag, frames):
    step = 256
    shape = jax.ShapeDtypeStruct((1, NI, NI), jnp.float32)
    out = pl.BlockSpec((1, step, NI), lambda i: (0, i, 0))
    vmem = pl.BlockSpec(memory_space=pltpu.VMEM)
    return pl.pallas_call(
        functools.partial(finish_kernel, frames, 4 * frames, step),
        out_shape=(shape, shape),
        grid=(NI // step,),
        in_specs=[vmem, vmem, vmem],
        out_specs=(out, out),
        compiler_params=pltpu.CompilerParams(vmem_limit_bytes=24 * 1024 * 1024),
        name="finish",
    )(last, real, imag)


def local(voltages):
    frames = voltages.shape[1] // FFT
    last, real, imag = exchange(voltages, pltpu.with_memory_space_constraint(jnp.asarray(tables()), pltpu.HBM))
    return finish(last, real, imag, frames)


def solution(mesh):
    return jax.shard_map(
        local,
        mesh=mesh,
        in_specs=(P("chan", "blk"),),
        out_specs=(P(("chan", "blk"), None, None), P(("chan", "blk"), None, None)),
        check_vma=False,
    )
```

time: 76.5 us -> 70 us (0.915)
  starting transfers between devices: 4.49 us -> 0 us
  local copies, waits for them, and re-layouts: 2.73 us -> 0 us
  Pallas kernels: 66.8 us -> 69.2 us
  waiting for transfers between devices: 1.62 us -> 0 us
    ppermute x1 -> x0, starting transfers between devices: 4.49 us -> none  [shifted(): lax.ppermute(value, axis, [(source, source + steps) for source in range(l...]
    pallas_call x1, Pallas kernels: 61.1 us -> 65.1 us  [exchange(): pl.pallas_call(functools.partial(exchange_kernel, frames), out_shape=(jax...]
    unnamed x4 -> x0, local copies, waits for them, and re-layouts: 1.83 us -> none
    ppermute x1 -> x0, waiting for transfers between devices: 1.62 us -> none  [shifted(): lax.ppermute(value, axis, [(source, source + steps) for source in range(l...]
    pallas_call x1, Pallas kernels: 5.67 us -> 4.11 us  [finish(): pl.pallas_call(functools.partial(finish_kernel, frames, 4 * frames, step)...]
    slice x1 -> x0, local copies, waits for them, and re-layouts: 0.9 us -> none  [local(): tail = voltages[:, (frames - HISTORY) * FFT:]]
  transfers between devices with their start and end apart: 1 -> 0, of which waited for: 1 -> 0; matrix products, arithmetic and copies ran while one was open for 0% -> 0% of each run, Pallas kernels for 0% -> 0%
where the time goes in v3:
time: 70 us; the launch traced here: 69.9 us
  Pallas kernels  69.2 us (99%)
    pallas_call x1, Pallas kernels, exchange(): pl.pallas_call(functools.partial(exchange_kernel, frames), out_shape=(jax...  65.1 us
    pallas_call x1, Pallas kernels, finish(): pl.pallas_call(functools.partial(finish_kernel, frames, 4 * frames, step)...  4.11 us

profile of v3, /device:TPU:1, one launch (start us, length us, event | category | flops | bytes accessed | tf_op | source)
XLA Modules:
  0.0 69.9 jit_solution(5409773715586309082)
XLA Ops:
  0.6 65.1 %filterbank_exchange.1 = (bf16[1024,256]{1,0:T(8,128)(2,1)S(1)}, f32[1024,1024]{1,0:T(8,128)S(1)}, f32[1024,1024]{1,0:T(8,128)S(1)}) custom-call(s32[16,65536]{1,0:T(8,128)} %v_hbm.1, f32[520,256]{1,0:T(8,128)} %constant.2.clone.table_hbm), custom_call_target="tpu_custom_call" | custom-call | tf_op jit(solution)/shard_map/filterbank_exchange/pallas_call | solution.py:314
  65.8 4.1 %finish.1 = (f32[1,1024,1024]{2,1,0:T(8,128)}, f32[1,1024,1024]{2,1,0:T(8,128)}) custom-call(bf16[1024,256]{1,0:T(8,128)(2,1)S(1)} %get-tuple-element.5.last_ref, f32[1024,1024]{1,0:T(8,128)S(1)} %get-tuple-element.6.re_in, f32[1024,1024]{1,0:T(8,128)S(1)} %get-tuple-element.7.im_in), custom_call_target="tpu_custom_call" | custom-call | tf_op jit(solution)/shard_map/finish/pallas_call | solution.py:360

commit v4 on v3

--- a/solution.py
+++ b/solution.py
@@ -57,6 +57,7 @@
     landed,
     in_sem,
     halo_sem,
+    plane_sem,
     send_sem,
     recv_sem,
 ):
@@ -88,20 +89,20 @@
 
     barrier = pltpu.get_barrier_semaphore()
 
+    mine = chan & ~7
+
+    def signal(semaphore, tc, tb):
+        pl.semaphore_signal(semaphore, inc=1, device_id=(tc, tb), device_id_type=MESH)
+
+    for dz in (4, 3, 5, 2, 6, 1, 7):
+        signal(barrier, mine | along[dz], blk)
+
     def greet(r, _):
-        base, tb = place((r & 3) ^ 2, ((r >> 2) & 3) ^ 2, r >> 4)
-        for dz in (4, 3, 5, 2, 6, 1, 7, 0):
-
-            def signal():
-                pl.semaphore_signal(barrier, inc=1, device_id=(base | along[dz], tb), device_id_type=MESH)
-
-            if dz:
-                signal()
-            else:
-                pl.when(r != 10)(signal)
+        base, tb = place(r & 3, (r >> 2) & 3, r >> 4)
+        signal(barrier, base | z, tb)
         return 0
 
-    lax.fori_loop(0, 32, greet, 0)
+    lax.fori_loop(1, 32, greet, 0)
 
     head[...] = jnp.zeros_like(head)
     table_load.wait()
@@ -234,7 +235,9 @@
     tail_out[...] = tail[...].astype(jnp.bfloat16)
     pairs = inputs // 2
     transform(0, core, 0, pairs // 2)
-    pl.semaphore_wait(barrier, 255)
+    pl.semaphore_wait(barrier, 38)
+    for dz in (4, 3, 5, 2, 6, 1, 7):
+        signal(plane_sem, mine | along[dz], blk)
     onward = pltpu.make_async_remote_copy(
         src_ref=tail_out,
         dst_ref=halo,
@@ -268,6 +271,8 @@
         for shift_x in range(2):
             phase = group * 2 + shift_x
             pack(phase, group, (blk >> 1) ^ shift_x)
+            if phase == 0:
+                pl.semaphore_wait(plane_sem, 7)
             send(phase)
 
     @pl.when(blk < blocks - 1)
@@ -331,6 +336,7 @@
             pltpu.VMEM((3, NI, 2 * frames), jnp.bfloat16),
             pltpu.SemaphoreType.DMA((chunks + 2,)),
             pltpu.SemaphoreType.DMA((2,)),
+            pltpu.SemaphoreType.REGULAR,
             pltpu.SemaphoreType.DMA,
             pltpu.SemaphoreType.DMA((4,)),
         ],

time: 70 us -> 67.9 us (0.970)
  Pallas kernels: 69.2 us -> 67.2 us
    pallas_call x1, Pallas kernels: 65.1 us -> 63 us  [exchange(): pl.pallas_call(functools.partial(exchange_kernel, frames), out_shape=(jax...]
where the time goes in v4:
time: 67.9 us; the launch traced here: 67.8 us
  Pallas kernels  67.2 us (99%)
    pallas_call x1, Pallas kernels, exchange(): pl.pallas_call(functools.partial(exchange_kernel, frames), out_shape=(jax...  63 us
    pallas_call x1, Pallas kernels, finish(): pl.pallas_call(functools.partial(finish_kernel, frames, 4 * frames, step)...  4.11 us

profile of v4, /device:TPU:1, one launch (start us, length us, event | category | flops | bytes accessed | tf_op | source)
XLA Modules:
  0.0 67.8 jit_solution(2532267559989758511)
XLA Ops:
  0.6 63.0 %filterbank_exchange.1 = (bf16[1024,256]{1,0:T(8,128)(2,1)S(1)}, f32[1024,1024]{1,0:T(8,128)S(1)}, f32[1024,1024]{1,0:T(8,128)S(1)}) custom-call(s32[16,65536]{1,0:T(8,128)} %v_hbm.1, f32[520,256]{1,0:T(8,128)} %constant.2.clone.table_hbm), custom_call_target="tpu_custom_call" | custom-call | tf_op jit(solution)/shard_map/filterbank_exchange/pallas_call | solution.py:319
  63.7 4.1 %finish.1 = (f32[1,1024,1024]{2,1,0:T(8,128)}, f32[1,1024,1024]{2,1,0:T(8,128)}) custom-call(bf16[1024,256]{1,0:T(8,128)(2,1)S(1)} %get-tuple-element.5.last_ref, f32[1024,1024]{1,0:T(8,128)S(1)} %get-tuple-element.6.re_in, f32[1024,1024]{1,0:T(8,128)S(1)} %get-tuple-element.7.im_in), custom_call_target="tpu_custom_call" | custom-call | tf_op jit(solution)/shard_map/finish/pallas_call | solution.py:366

commit v5 on v4

--- a/solution.py
+++ b/solution.py
@@ -209,8 +209,9 @@
             pltpu.make_async_copy(spec.at[0, chan], landing(0).at[row, :], recv_sem.at[0]).start()
 
         def body(r, _):
-            base, tb = place(shift_x + 2 * (r & 1), r >> 1, shift_core)
-            for dz in (1, 7, 2, 6, 3, 5, 4, 0):
+            q = r ^ 5
+            base, tb = place(shift_x + 2 * (q & 1), q >> 1, shift_core)
+            for dz in (4, 3, 5, 2, 6, 1, 7, 0):
                 tc = base | along[dz]
 
                 def copy():
@@ -226,7 +227,7 @@
                 if dz or phase:
                     copy()
                 else:
-                    pl.when(r > 0)(copy)
+                    pl.when(q > 0)(copy)
             return 0
 
         lax.fori_loop(0, 8, body, 0)

time: 67.9 us -> 69.7 us (1.027)
  Pallas kernels: 67.2 us -> 68.9 us
    pallas_call x1, Pallas kernels: 63 us -> 64.8 us  [exchange(): pl.pallas_call(functools.partial(exchange_kernel, frames), out_shape=(jax...]
where the time goes in v5:
time: 69.7 us; the launch traced here: 69.6 us
  Pallas kernels  68.9 us (99%)
    pallas_call x1, Pallas kernels, exchange(): pl.pallas_call(functools.partial(exchange_kernel, frames), out_shape=(jax...  64.8 us
    pallas_call x1, Pallas kernels, finish(): pl.pallas_call(functools.partial(finish_kernel, frames, 4 * frames, step)...  4.11 us

profile of v5, /device:TPU:1, one launch (start us, length us, event | category | flops | bytes accessed | tf_op | source)
XLA Modules:
  0.0 69.6 jit_solution(17710249071940326180)
XLA Ops:
  0.6 64.8 %filterbank_exchange.1 = (bf16[1024,256]{1,0:T(8,128)(2,1)S(1)}, f32[1024,1024]{1,0:T(8,128)S(1)}, f32[1024,1024]{1,0:T(8,128)S(1)}) custom-call(s32[16,65536]{1,0:T(8,128)} %v_hbm.1, f32[520,256]{1,0:T(8,128)} %constant.2.clone.table_hbm), custom_call_target="tpu_custom_call" | custom-call | tf_op jit(solution)/shard_map/filterbank_exchange/pallas_call | solution.py:320
  65.5 4.1 %finish.1 = (f32[1,1024,1024]{2,1,0:T(8,128)}, f32[1,1024,1024]{2,1,0:T(8,128)}) custom-call(bf16[1024,256]{1,0:T(8,128)(2,1)S(1)} %get-tuple-element.5.last_ref, f32[1024,1024]{1,0:T(8,128)S(1)} %get-tuple-element.6.re_in, f32[1024,1024]{1,0:T(8,128)S(1)} %get-tuple-element.7.im_in), custom_call_target="tpu_custom_call" | custom-call | tf_op jit(solution)/shard_map/finish/pallas_call | solution.py:367

commit v6 on v4

--- a/solution.py
+++ b/solution.py
@@ -210,7 +210,7 @@
 
         def body(r, _):
             base, tb = place(shift_x + 2 * (r & 1), r >> 1, shift_core)
-            for dz in (1, 7, 2, 6, 3, 5, 4, 0):
+            for dz in (0, 1, 2, 3, 4, 5, 6, 7):
                 tc = base | along[dz]
 
                 def copy():

time: 67.9 us -> 67.9 us (level)
  no operation moved by 1% of the time
where the time goes in v6:
time: 67.9 us; the launch traced here: 67.8 us
  Pallas kernels  67.2 us (99%)
    pallas_call x1, Pallas kernels, exchange(): pl.pallas_call(functools.partial(exchange_kernel, frames), out_shape=(jax...  63.1 us
    pallas_call x1, Pallas kernels, finish(): pl.pallas_call(functools.partial(finish_kernel, frames, 4 * frames, step)...  4.11 us

profile of v6, /device:TPU:1, one launch (start us, length us, event | category | flops | bytes accessed | tf_op | source)
XLA Modules:
  0.0 67.8 jit_solution(7343176220786116120)
XLA Ops:
  0.6 63.1 %filterbank_exchange.1 = (bf16[1024,256]{1,0:T(8,128)(2,1)S(1)}, f32[1024,1024]{1,0:T(8,128)S(1)}, f32[1024,1024]{1,0:T(8,128)S(1)}) custom-call(s32[16,65536]{1,0:T(8,128)} %v_hbm.1, f32[520,256]{1,0:T(8,128)} %constant.2.clone.table_hbm), custom_call_target="tpu_custom_call" | custom-call | tf_op jit(solution)/shard_map/filterbank_exchange/pallas_call | solution.py:319
  63.7 4.1 %finish.1 = (f32[1,1024,1024]{2,1,0:T(8,128)}, f32[1,1024,1024]{2,1,0:T(8,128)}) custom-call(bf16[1024,256]{1,0:T(8,128)(2,1)S(1)} %get-tuple-element.5.last_ref, f32[1024,1024]{1,0:T(8,128)S(1)} %get-tuple-element.6.re_in, f32[1024,1024]{1,0:T(8,128)S(1)} %get-tuple-element.7.im_in), custom_call_target="tpu_custom_call" | custom-call | tf_op jit(solution)/shard_map/finish/pallas_call | solution.py:366
